TPU v7x, 32 devices: a whole 2x2x4 slice. The times are simulated.
32 devices in a mesh: seq: 8 (over z, y), tp: 4 (over x, core).
Axes of the slice: x: 2, y: 2, z: 4, core: 2. Of those that a mesh axis runs over, the one named last changes fastest.
Arguments:
- tokens: bfloat16 [8192, 1152], P('seq', 'tp'), may hold values from -6 to 6
- out_grad: bfloat16 [8192, 1152], P('seq', 'tp'), may hold values from -6 to 6
- route_mask: int32 [8192], P('seq'), may hold values from 0 to 1, as said below
- kept_counts: int32 [32], replicated, may hold values from 64 to 192, as said below
- labels: int32 [32], replicated, may hold values from 0 to 1000
- timesteps: int32 [32], replicated, may hold values from 0 to 999
- class_table: bfloat16 [1001, 1152], replicated, may hold values from -6 to 6
- ada_weight: bfloat16 [1152, 6, 1152], P(None, None, 'tp'), may hold values from -0.1875 to 0.1875
- ada_bias: bfloat16 [6, 1152], P(None, 'tp'), may hold values from -2 to 2
- qkv_weight: bfloat16 [1152, 3, 1152], P(None, None, 'tp'), may hold values from -0.1875 to 0.1875
- qv_bias: bfloat16 [2, 1152], P(None, 'tp'), may hold values from -2 to 2
- proj_weight: bfloat16 [1152, 1152], P('tp'), may hold values from -0.5 to 0.5
- proj_bias: bfloat16 [1152], P('tp'), may hold values from -2 to 2
- hidden_weight: bfloat16 [1152, 4608], P(None, 'tp'), may hold values from -0.1875 to 0.1875
- hidden_bias: bfloat16 [4608], P('tp'), may hold values from -2 to 2
- output_weight: bfloat16 [4608, 1152], P('tp'), may hold values from -0.09375 to 0.09375
- output_bias: bfloat16 [1152], P('tp'), may hold values from -2 to 2
Outputs:
- output: bfloat16 [8192, 1152], P('seq', 'tp')
- tokens_grad: bfloat16 [8192, 1152], P('seq', 'tp')
- class_grad: float32 [1001, 1152], P(None, 'seq')
- ada_weight_grad: float32 [1152, 6, 1152], P('seq', None, 'tp')
- ada_bias_grad: float32 [6, 1152], P(None, 'tp')
- qkv_weight_grad: float32 [1152, 3, 1152], P('seq', None, 'tp')
- qv_bias_grad: float32 [2, 1152], P(None, 'tp')
- proj_weight_grad: float32 [1152, 1152], P('tp', 'seq')
- proj_bias_grad: float32 [1152], P('tp')
- hidden_weight_grad: float32 [1152, 4608], P('seq', 'tp')
- hidden_bias_grad: float32 [4608], P('tp')
- output_weight_grad: float32 [4608, 1152], P('tp', 'seq')
- output_bias_grad: float32 [1152], P('tp')
Inputs may be any that keep to these rules, and one draw needn't show every extreme that they name: route_mask keeps exactly kept_counts[i] of the 256 tokens of image i. The kept tokens of all images number 512 * 8; the kept tokens of the first j * 4 images exceed j * 512 by 0 to 128 for every j, by exactly 128 for some j, and by 0 at the end. Every aligned block of 4 images has one image with 192 kept tokens. `route_mask`: consistent with kept_counts.
All inputs are finite; a program needn't handle non-finite values.
Results may differ from a plain program's by a relative error of at most 0.025.
The roundings to bfloat16 on the way count: a program that leaves them out, or rounds other values in their place, can miss the bound.
Values may be sent and summed in bfloat16 or wider, within the bound.
A program may use at most 192 MiB of HBM per device.

v0:
```python
import math
import jax
import jax.numpy as jnp
from jax import lax
from jax.sharding import PartitionSpec as P

HEAD_DIM = 72
IMG_DEV = 4
ROWS = 640
NORM_EPS = 1e-06
HIGHEST = lax.Precision.HIGHEST


def exact_dot(left_mat, right_mat):
    return jnp.dot(left_mat, right_mat, precision=HIGHEST, preferred_element_type=jnp.float32)


def time_embed(step_ids, model_width):
    half_width = model_width // 2
    frequency = jnp.exp(-math.log(10000.0) * jnp.arange(half_width, dtype=jnp.float32) / half_width)
    angles = step_ids.astype(jnp.float32)[:, None] * frequency[None, :]
    return jnp.concatenate([jnp.cos(angles), jnp.sin(angles)], axis=1)


def norm_rows(values):
    centered = values - jnp.mean(values, axis=1, keepdims=True)
    inverse = lax.rsqrt(jnp.mean(centered * centered, axis=1, keepdims=True) + NORM_EPS)
    return (centered * inverse, inverse)


def gelu_tanh(values):
    return jax.nn.gelu(values, approximate=True)


def local(
    tokens,
    out_grad,
    route_mask,
    kept_counts,
    labels,
    timesteps,
    class_table,
    ada_weight,
    ada_bias,
    qkv_weight,
    qv_bias,
    proj_weight,
    proj_bias,
    hidden_weight,
    hidden_bias,
    output_weight,
    output_bias,
):
    f32, bf16 = (jnp.float32, jnp.bfloat16)
    seq_index = lax.axis_index("seq")
    tp_index = lax.axis_index("tp")
    seq_size = lax.axis_size("seq")
    col_local = tokens.shape[1]
    model_width = class_table.shape[1]
    head_cols = qkv_weight.shape[2]
    heads_local = head_cols // HEAD_DIM
    slice_width = model_width // seq_size
    images = kept_counts.shape[0]
    scale_factor = HEAD_DIM ** (-0.5)
    col_start = tp_index * col_local
    first_image = seq_index * IMG_DEV
    own_counts = lax.dynamic_slice_in_dim(kept_counts, first_image, IMG_DEV)
    own_ends = jnp.cumsum(own_counts)
    rank = jnp.where(route_mask > 0, jnp.cumsum(route_mask) - 1, -1)
    row_ids = jnp.arange(ROWS, dtype=jnp.int32)
    place = (rank[None, :] == row_ids[:, None]).astype(bf16)
    row_image = jnp.sum((own_ends[None, :] <= row_ids[:, None]).astype(jnp.int32), axis=1)
    row_onehot = (row_image[:, None] == jnp.arange(IMG_DEV, dtype=jnp.int32)[None, :]).astype(f32)

    def whole_rows(part_rows):
        return lax.all_gather(part_rows, "tp", axis=1, tiled=True)

    def column_sum(part_rows):
        return lax.psum_scatter(
            part_rows.astype(bf16), "tp", scatter_dimension=1, tiled=True
        ).astype(f32)

    def own_cols(full_rows):
        return lax.dynamic_slice_in_dim(full_rows, col_start, col_local, 1)

    def reinsert(rows_new, initial):
        placed = jnp.einsum("rt,rc->tc", place, rows_new, preferred_element_type=f32).astype(bf16)
        return jnp.where(route_mask[:, None] > 0, placed, initial)

    label_hot = (
        labels[:, None] == jnp.arange(class_table.shape[0], dtype=jnp.int32)[None, :]
    ).astype(bf16)
    condition = jnp.dot(label_hot, class_table, preferred_element_type=f32) + time_embed(
        timesteps, model_width
    )
    cond_low = jax.nn.silu(condition).astype(bf16)
    cond_own = lax.dynamic_slice_in_dim(cond_low, first_image, IMG_DEV)
    mod_own = (
        jnp.einsum("wd,dcf->wcf", cond_own, ada_weight, preferred_element_type=f32)
        + ada_bias.astype(f32)[None]
    )
    mod_full = lax.all_gather(mod_own, "tp", axis=2, tiled=True)

    def row_full(stretch_id):
        return exact_dot(row_onehot, mod_full[:, stretch_id, :])

    def row_own(stretch_id):
        return exact_dot(row_onehot, mod_own[:, stretch_id, :])

    def input_grads(partial_rows, normed, inverse, scale):
        own_grad = column_sum(partial_rows)
        normed_own = own_cols(normed)
        scaled_grad = own_grad * (1.0 + own_cols(scale))
        mean_grad, mean_cross = lax.psum(
            (
                jnp.sum(scaled_grad, axis=1, keepdims=True) / model_width,
                jnp.sum(scaled_grad * normed_own, axis=1, keepdims=True) / model_width,
            ),
            "tp",
        )
        return (
            own_grad,
            own_grad * normed_own,
            inverse * (scaled_grad - mean_grad - normed_own * mean_cross),
        )

    picked = jnp.dot(place, jnp.concatenate([tokens, out_grad], axis=1), preferred_element_type=f32)
    rows_in = picked[:, :col_local].astype(bf16)
    grad_rows = picked[:, col_local:]
    gate_one = row_own(2)
    gate_two = row_own(5)
    mlp_grad = (grad_rows * gate_two).astype(bf16)
    full_in = whole_rows(rows_in).astype(f32)
    mlp_grad_full = whole_rows(mlp_grad)
    normed_one, inverse_one = norm_rows(full_in)
    scale_one = row_full(1)
    branch_one = (normed_one * (1.0 + scale_one) + row_full(0)).astype(bf16)
    qkv_bias = jnp.stack([qv_bias[0], jnp.zeros_like(qv_bias[0]), qv_bias[1]]).astype(f32)
    qkv_rows = (
        jnp.einsum("rd,dcf->rcf", branch_one, qkv_weight, preferred_element_type=f32)
        + qkv_bias[None]
    ).astype(bf16)
    query_all, key_all, value_all = (
        qkv_rows[:, part].reshape(ROWS, heads_local, HEAD_DIM) for part in range(3)
    )
    same_image = row_image[:, None] == row_image[None, :]
    raw = jnp.einsum("qhe,khe->hqk", query_all, key_all, preferred_element_type=f32) * scale_factor
    masked = jnp.where(same_image[None], raw, -1e30)
    top_score = jnp.max(masked, axis=2, keepdims=True)
    exp_scores = jnp.exp(masked - top_score)
    attn_probs = exp_scores / jnp.sum(exp_scores, axis=2, keepdims=True)
    probs_low = attn_probs.astype(bf16)
    attended = (
        jnp.einsum("hqk,khe->qhe", probs_low, value_all, preferred_element_type=f32)
        .reshape(ROWS, head_cols)
        .astype(bf16)
    )
    attn_out = column_sum(
        jnp.dot(attended, proj_weight, preferred_element_type=f32)
    ) + proj_bias.astype(f32)
    middle = rows_in.astype(f32) + gate_one * attn_out
    middle_full = whole_rows(middle.astype(bf16)).astype(f32)
    normed_two, inverse_two = norm_rows(middle_full)
    scale_two = row_full(4)
    branch_two = (normed_two * (1.0 + scale_two) + row_full(3)).astype(bf16)
    pre_act = jnp.dot(branch_two, hidden_weight, preferred_element_type=f32) + hidden_bias.astype(
        f32
    )
    act_low = gelu_tanh(pre_act).astype(bf16)
    mlp_out = column_sum(
        jnp.dot(act_low, output_weight, preferred_element_type=f32)
    ) + output_bias.astype(f32)
    final_rows = middle + gate_two * mlp_out
    output = reinsert(final_rows.astype(bf16), tokens)
    gate_two_rows = grad_rows * mlp_out
    output_bias_term = jnp.sum(mlp_grad, axis=0, dtype=f32)
    output_weight_term = jnp.einsum(
        "rf,rd->fd", act_low, mlp_grad_full, preferred_element_type=f32
    ).astype(bf16)
    act_grad = jnp.einsum("rd,fd->rf", mlp_grad_full, output_weight, preferred_element_type=f32)
    gelu_pull = jax.vjp(gelu_tanh, pre_act)[1]
    pre_grad = gelu_pull(act_grad)[0].astype(bf16)
    hidden_bias_term = jnp.sum(pre_grad, axis=0, dtype=f32)
    hidden_weight_term = jnp.einsum(
        "rd,rf->df", branch_two, pre_grad, preferred_element_type=f32
    ).astype(bf16)
    two_partial = jnp.einsum("rf,df->rd", pre_grad, hidden_weight, preferred_element_type=f32)
    shift_two_grad, scale_two_grad, two_norm_grad = input_grads(
        two_partial, normed_two, inverse_two, scale_two
    )
    middle_grad = grad_rows + two_norm_grad
    gate_one_rows = middle_grad * attn_out
    attn_grad = (middle_grad * gate_one).astype(bf16)
    proj_bias_term = jnp.sum(attn_grad, axis=0, dtype=f32)
    attn_grad_full = whole_rows(attn_grad)
    proj_weight_term = jnp.einsum(
        "rf,rd->fd", attended, attn_grad_full, preferred_element_type=f32
    ).astype(bf16)
    attended_grad = (
        jnp.einsum("rd,fd->rf", attn_grad_full, proj_weight, preferred_element_type=f32)
        .astype(bf16)
        .reshape(ROWS, heads_local, HEAD_DIM)
    )
    value_term = jnp.einsum("hqk,qhe->khe", probs_low, attended_grad, preferred_element_type=f32)
    prob_grad = jnp.einsum("qhe,khe->hqk", attended_grad, value_all, preferred_element_type=f32)
    row_dot = jnp.sum(attn_probs * prob_grad, axis=2, keepdims=True)
    score_grad = (attn_probs * (prob_grad - row_dot)).astype(bf16)
    query_term = (
        jnp.einsum("hqk,khe->qhe", score_grad, key_all, preferred_element_type=f32) * scale_factor
    )
    key_term = (
        jnp.einsum("hqk,qhe->khe", score_grad, query_all, preferred_element_type=f32) * scale_factor
    )
    qkv_grad = (
        jnp.stack([query_term, key_term, value_term], axis=1)
        .reshape(ROWS, 3, head_cols)
        .astype(bf16)
    )
    qkv_sums = jnp.sum(qkv_grad, axis=0, dtype=f32)
    qkv_weight_term = jnp.einsum(
        "rd,rcf->dcf", branch_one, qkv_grad, preferred_element_type=f32
    ).astype(bf16)
    one_partial = jnp.einsum("rcf,dcf->rd", qkv_grad, qkv_weight, preferred_element_type=f32)
    shift_one_grad, scale_one_grad, one_norm_grad = input_grads(
        one_partial, normed_one, inverse_one, scale_one
    )
    in_grad = middle_grad + one_norm_grad
    tokens_grad = reinsert(in_grad.astype(bf16), out_grad)
    per_row = jnp.concatenate(
        [
            shift_one_grad,
            scale_one_grad,
            gate_one_rows,
            shift_two_grad,
            scale_two_grad,
            gate_two_rows,
        ],
        axis=1,
    )
    mod_grad = jnp.einsum(
        "rw,rf->wf", row_onehot, per_row, precision=HIGHEST, preferred_element_type=f32
    )
    small = jnp.concatenate(
        [
            mod_grad.reshape(-1),
            qkv_sums[0],
            qkv_sums[2],
            proj_bias_term,
            hidden_bias_term,
            output_bias_term,
        ]
    )
    small_all = lax.all_gather(small, "seq", axis=0)
    mod_size = mod_grad.size
    mod_all = small_all[:, :mod_size].reshape(images, 6, col_local)
    bias_sums = jnp.sum(small_all[:, mod_size:], axis=0)
    ada_bias_grad = jnp.sum(mod_all, axis=0)
    qv_bias_grad = bias_sums[: 2 * col_local].reshape(2, col_local)
    at = 2 * col_local
    proj_bias_grad = bias_sums[at : at + col_local]
    at += col_local
    hidden_bias_grad = bias_sums[at : at + hidden_bias.shape[0]]
    at += hidden_bias.shape[0]
    output_bias_grad = bias_sums[at:]
    width_start = seq_index * slice_width
    cond_cols = lax.dynamic_slice_in_dim(condition, width_start, slice_width, 1)
    low_cols = lax.dynamic_slice_in_dim(cond_low, width_start, slice_width, 1)
    ada_weight_grad = jnp.einsum(
        "wd,wcf->dcf", low_cols.astype(f32), mod_all, precision=HIGHEST, preferred_element_type=f32
    )
    ada_rows = lax.dynamic_slice_in_dim(ada_weight, width_start, slice_width, 0)
    cond_grad = lax.psum(
        jnp.einsum(
            "wcf,dcf->wd",
            mod_all,
            ada_rows.astype(f32),
            precision=HIGHEST,
            preferred_element_type=f32,
        ),
        "tp",
    )
    silu_pull = jax.vjp(jax.nn.silu, cond_cols)[1]
    class_grad = jnp.einsum(
        "wc,wd->cd",
        label_hot.astype(f32),
        silu_pull(cond_grad)[0],
        precision=HIGHEST,
        preferred_element_type=f32,
    )
    qkv_weight_grad, proj_weight_grad, hidden_weight_grad, output_weight_grad = (
        lax.psum_scatter(qkv_weight_term, "seq", scatter_dimension=0, tiled=True).astype(f32),
        lax.psum_scatter(proj_weight_term, "seq", scatter_dimension=1, tiled=True).astype(f32),
        lax.psum_scatter(hidden_weight_term, "seq", scatter_dimension=0, tiled=True).astype(f32),
        lax.psum_scatter(output_weight_term, "seq", scatter_dimension=1, tiled=True).astype(f32),
    )
    return (
        output,
        tokens_grad,
        class_grad,
        ada_weight_grad,
        ada_bias_grad,
        qkv_weight_grad,
        qv_bias_grad,
        proj_weight_grad,
        proj_bias_grad,
        hidden_weight_grad,
        hidden_bias_grad,
        output_weight_grad,
        output_bias_grad,
    )


def solution(mesh):
    return jax.shard_map(
        local,
        mesh=mesh,
        in_specs=(
            P("seq", "tp"),
            P("seq", "tp"),
            P("seq"),
            P(),
            P(),
            P(),
            P(),
            P(None, None, "tp"),
            P(None, "tp"),
            P(None, None, "tp"),
            P(None, "tp"),
            P("tp", None),
            P("tp"),
            P(None, "tp"),
            P("tp"),
            P("tp", None),
            P("tp"),
        ),
        out_specs=(
            P("seq", "tp"),
            P("seq", "tp"),
            P(None, "seq"),
            P("seq", None, "tp"),
            P(None, "tp"),
            P("seq", None, "tp"),
            P(None, "tp"),
            P("tp", "seq"),
            P("tp"),
            P("seq", "tp"),
            P("tp"),
            P("tp", "seq"),
            P("tp"),
        ),
        check_vma=False,
    )
```

profile of v0, /device:TPU:0, one launch (start us, length us, event | category | flops | bytes accessed | tf_op | source)
XLA Modules:
  0.0 589.2 jit_solution(4795627765267242598)
XLA Ops:
  9.4 2.4 fusion.24
  14.4 2.9 multiply_convert_fusion.4
  17.3 3.5 convolution_add_fusion.4
  21.1 26.5 %all_gather.22 = f32[4,6,1152]{1,0,2:T(4,128)S(1)} all-gather(f32[4,6,288]{1,0,2:T(4,128)S(1)} %copy.102), channel_id=1, replica_groups=mesh['seq'=8,'tp'=4] {'tp'}, dimensions={2}, use_global_device_ids=true | all-gather | bytes 138240 | tf_op jit(solution)/shard_map/all_gather | solution.py:102
  47.6 6.0 %fusion.109 = (f32[4,1,1152]{1,0,2:T(4,128)}, f32[4,1,1152]{1,0,2:T(4,128)}, f32[4,1,1152]{1,0,2:T(4,128)}, f32[4,1,1152]{1,0,2:T(4,128)}) fusion(f32[4,6,1152]{1,0,2:T(4,128)S(1)} %all_gather.22), kind=kLoop, calls=%fused_computation.184 | loop fusion | bytes 147456 | tf_op jit(solution)/shard_map/slice | solution.py:105
  53.6 2.1 copy.105
  55.7 2.3 copy.103
  59.4 3.1 fusion.59
  62.5 1.8 convert_reduce_fusion.1
  64.2 1.8 fusion.13
  66.1 3.9 fusion.21
  70.0 1.9 add_convert_fusion
  72.7 6.5 %fusion.113 = (f32[4,640]{1,0:T(4,128)S(1)}, f32[4,640,640]{1,2,0:T(8,128)}) fusion(pred[640,640]{0,1:T(8,128)(4,1)} %broadcast_compare_fusion, bf16[640,4,72]{0,2,1:T(8,128)(2,1)S(1)} %bitcast.99, bf16[640,4,72]{0,2,1:T(8,128)(2,1)S(1)} %bitcast.97), kind=kOutput, calls=%fused_computation.188 | convolution fusion | flops 242483840 | bytes 7710720 | tf_op jit(solution)/shard_map/sub | solution.py:150
  79.2 3.7 fusion.38
  83.7 2.2 convolution_convert_fusion.5
  85.9 2.7 convert_reduce_fusion.4
  88.8 25.1 %reduce-scatter.9.cloned.1.call-done = bf16[640,288]{0,1:T(8,128)(2,1)} async-done(((bf16[640,1152]{0,1:T(8,128)(2,1)}), bf16[640,288]{0,1:T(8,128)(2,1)}) %reduce-scatter.9.cloned.1.call-update) | async-done | bytes 368656 | tf_op jit(solution)/shard_map/reduce_scatter | solution.py:79
  113.9 2.9 fusion.78
  116.9 2.1 copy.111
  119.0 2.3 copy.109
  121.3 3.1 fusion.57
  124.4 10.8 %all-gather.10.cloned.1.call-done = bf16[640,1152]{0,1:T(8,128)(2,1)} async-done(((bf16[640,288]{0,1:T(8,128)(2,1)}), bf16[640,1152]{0,1:T(8,128)(2,1)}) %all-gather.10.cloned.1.call-update) | async-done | bytes 1474576 | tf_op jit(solution)/shard_map/all_gather | solution.py:76
  135.2 6.1 %fusion.115 = f32[640,1152]{0,1:T(8,128)} fusion(bf16[1152,1152]{1,0:T(8,128)(2,1)} %param.32, bf16[640,1152]{0,1:T(8,128)(2,1)} %all-gather.10.cloned.1.call-done), kind=kOutput, calls=%fused_computation.190 | convolution fusion | flops 1698693120 | bytes 7077888 | tf_op jit(solution)/shard_map/rd,fd->rf/dot_general | solution.py:180
  141.3 15.1 %all-gather.8.cloned.1.call-done = bf16[640,1152]{0,1:T(8,128)(2,1)} async-done(((bf16[640,288]{0,1:T(8,128)(2,1)}), bf16[640,1152]{0,1:T(8,128)(2,1)}) %all-gather.8.cloned.1.call-update) | async-done | bytes 1474576 | tf_op jit(solution)/shard_map/all_gather | solution.py:76
  156.4 1.8 convert_reduce_fusion
  158.2 1.8 fusion.12
  160.0 3.9 fusion.11
  164.0 6.0 %convert_reduce_fusion.2 = (f32[1152]{0:T(1024)S(1)}, bf16[640,1152]{0,1:T(8,128)(2,1)S(1)}, f32[640,1152]{0,1:T(8,128)}) fusion(f32[640,1152]{0,1:T(8,128)S(1)} %copy-done.43, f32[1152]{0:T(1024)S(1)} %convert_element_type.178, bf16[640,1152]{0,1:T(8,128)(2,1)S(1)} %fusion.11, bf16[1152,1152]{1,0:T(8,128)(2,1)S(1)} %copy-done), kind=kOutput, calls=%fused_computation.42 | convolution fusion | flops 1715649408 | bytes 11510784 | tf_op jit(solution)/shard_map/dot_general | solution.py:166
  171.2 4.0 convolution_convert_fusion.3
  175.2 3.4 fusion.4
  178.6 24.3 %reduce-scatter.13.cloned.1.call-done = bf16[640,288]{0,1:T(8,128)(2,1)} async-done(((bf16[640,1152]{0,1:T(8,128)(2,1)}), bf16[640,288]{0,1:T(8,128)(2,1)}) %reduce-scatter.13.cloned.1.call-update) | async-done | bytes 368656 | tf_op jit(solution)/shard_map/reduce_scatter | solution.py:79
  204.3 5.9 all-reduce.1
  210.2 2.9 convert_reduce_fusion.5
  213.2 6.6 %convolution_convert_fusion.4 = bf16[640,1152]{0,1:T(8,128)(2,1)} fusion(bf16[1152,1152]{1,0:T(8,128)(2,1)} %param.32, f32[640,1152]{0,1:T(8,128)} %get-tuple-element.54), kind=kOutput, calls=%fused_computation.28 | convolution fusion | flops 1706065920 | bytes 7077888 | tf_op jit(solution)/shard_map/dot_general | solution.py:171
  219.8 5.4 convolution_convert_fusion.1
  225.3 5.8 convolution_convert_fusion
  231.4 2.1 all-gather.12.cloned.1.call-done
  233.5 2.4 convolution_convert_fusion.7
  236.0 1.9 convolution_convert_fusion.6
  237.9 4.1 multiply_reduce_fusion
  244.0 2.0 fusion.37
  246.1 1.7 fusion.36
  247.9 4.3 fusion.41
  252.2 3.2 fusion.9
  255.8 1.9 fusion.2
  257.7 5.6 convolution_convert_fusion.2
  263.7 3.2 fusion.35
  267.2 71.5 %reduce-scatter.21.cloned.1.call-done = bf16[144,1152]{1,0:T(8,128)(2,1)} async-done(((bf16[1152,1152]{1,0:T(8,128)(2,1)}), bf16[144,1152]{1,0:T(8,128)(2,1)}) %reduce-scatter.21.cloned.1.call-update) | async-done | bytes 331792 | tf_op jit(solution)/shard_map/reduce_scatter | solution.py:293
  338.7 1.9 convert_element_type.205
  340.5 71.4 %reduce-scatter.23.cloned.1.call-done = bf16[1152,144]{0,1:T(8,128)(2,1)} async-done(((bf16[1152,1152]{0,1:T(8,128)(2,1)}), bf16[1152,144]{0,1:T(8,128)(2,1)}) %reduce-scatter.23.cloned.1.call-update) | async-done | bytes 331792 | tf_op jit(solution)/shard_map/reduce_scatter | solution.py:294
  412.0 1.9 convert_element_type.207
  413.8 62.3 %reduce-scatter.19.cloned.1.call-done = bf16[288,144]{0,1:T(8,128)(2,1)} async-done(((bf16[288,1152]{0,1:T(8,128)(2,1)}), bf16[288,144]{0,1:T(8,128)(2,1)}) %reduce-scatter.19.cloned.1.call-update) | async-done | bytes 82960 | tf_op jit(solution)/shard_map/reduce_scatter | solution.py:292
  476.1 1.6 convert_element_type.203
  477.7 27.7 %reduce-scatter.15.cloned.1.call-done = bf16[640,288]{0,1:T(8,128)(2,1)} async-done(((bf16[640,1152]{0,1:T(8,128)(2,1)}), bf16[640,288]{0,1:T(8,128)(2,1)}) %reduce-scatter.15.cloned.1.call-update) | async-done | bytes 368656 | tf_op jit(solution)/shard_map/reduce_scatter | solution.py:79
  506.4 1.6 fusion.75
  509.6 2.3 fusion.64
  512.1 31.6 %all-gather = f32[73728]{0:T(1024)S(1)} all-gather(f32[9216]{0:T(1024)S(1)} %concatenate.21), channel_id=2, replica_groups=mesh['seq'=8,'tp'=4] {'seq'}, dimensions={0}, use_global_device_ids=true | all-gather | bytes 331776 | tf_op jit(solution)/shard_map/all_gather | solution.py:253
  546.1 2.0 convolution_bitcast_fusion.1
  548.1 11.1 %all-reduce = (f32[640]{0:T(1024)S(1)}, f32[640]{0:T(1024)S(1)}, f32[32,144]{1,0:T(8,128)S(1)}) all-reduce(f32[640]{0:T(1024)S(1)} %broadcast_multiply_fusion, f32[640]{0:T(1024)S(1)} %broadcast_multiply_fusion.1, f32[32,144]{1,0:T(8,128)S(1)} %convolution_bitcast_fusion.1), channel_id=1, replica_groups=mesh['seq'=8,'tp'=4] {'tp'}, use_global_device_ids=true, to_apply=%region_22.23 | all-reduce | flops 5888 | bytes 47104 | tf_op jit(solution)/shard_map/psum | solution.py:114
  559.9 2.1 fusion.73
  562.0 1.8 fusion.61
  563.9 3.5 fusion.34
  567.3 12.9 %reduce-scatter.17.cloned.1.call-done = bf16[144,3,288]{2,0,1:T(8,128)(2,1)} async-done(((bf16[1152,3,288]{2,0,1:T(8,128)(2,1)}), bf16[144,3,288]{2,0,1:T(8,128)(2,1)}) %reduce-scatter.17.cloned.1.call-update) | async-done | bytes 248848 | tf_op jit(solution)/shard_map/reduce_scatter | solution.py:291
  580.2 1.9 convert_element_type.201
  (170 shorter events, 20.0 us)
Async XLA Ops:
  7.2 156.8 %copy-start = (bf16[1152,1152]{1,0:T(8,128)(2,1)S(1)}, bf16[1152,1152]{1,0:T(8,128)(2,1)}, u32[]{:S(2)}) copy-start(bf16[1152,1152]{1,0:T(8,128)(2,1)} %param.30) | copy-start | bytes 7962628
  7.2 55.3 %all-gather.6.cloned.1.call-start = ((), (), s32[]{:S(2)}) async-start(), calls=%async_computation.8 | async-start | bytes 1843200 | tf_op jit(solution)/shard_map/all_gather | solution.py:76
  9.3 4.4 copy-start.37
  9.3 4.7 copy-start.38
  9.3 4.7 copy-start.27
  9.3 5.1 copy-start.29
  11.8 1.1 copy-start.6
  13.7 100.2 %reduce-scatter.9.cloned.1.call-start = ((), (), s32[]{:S(2)}) async-start(), calls=%async_computation.9 | async-start | bytes 1843200 | tf_op jit(solution)/shard_map/reduce_scatter | solution.py:79
  53.6 4.6 copy-start.26
  62.5 3.6 copy-start.2
  66.1 3.9 copy-start.32
  70.0 1.9 copy-start.11
  72.7 6.5 %copy-start.16 = (bf16[640,1,288]{0,2,1:T(8,128)(2,1)}, bf16[640,1,288]{0,2,1:T(8,128)(2,1)S(1)}, u32[]{:S(2)}) copy-start(bf16[640,1,288]{0,2,1:T(8,128)(2,1)S(1)} %get-tuple-element.38) | copy-start | bytes 1105924
  72.7 6.5 %copy-start.17 = (bf16[640,1,288]{0,2,1:T(8,128)(2,1)}, bf16[640,1,288]{0,2,1:T(8,128)(2,1)S(1)}, u32[]{:S(2)}) copy-start(bf16[640,1,288]{0,2,1:T(8,128)(2,1)S(1)} %get-tuple-element.39) | copy-start | bytes 1105924
  79.2 4.5 copy-start.36
  82.9 0.7 copy-start.39
  83.7 5.1 copy-start.30
  85.9 31.0 %copy-start.28 = (bf16[1152]{0:T(1024)(128)(2,1)S(1)}, bf16[1152]{0:T(1024)(128)(2,1)}, u32[]{:S(2)}) copy-start(bf16[1152]{0:T(1024)(128)(2,1)} %param.31) | copy-start | bytes 6916
  85.9 49.3 %all-gather.10.cloned.1.call-start = ((), (), s32[]{:S(2)}) async-start(), calls=%async_computation.12 | async-start | bytes 1843200 | tf_op jit(solution)/shard_map/all_gather | solution.py:76
  88.7 67.7 %all-gather.8.cloned.1.call-start = ((), (), s32[]{:S(2)}) async-start(), calls=%async_computation.10 | async-start | bytes 1843200 | tf_op jit(solution)/shard_map/all_gather | solution.py:76
  116.8 86.1 %reduce-scatter.13.cloned.1.call-start = ((), (), s32[]{:S(2)}) async-start(), calls=%async_computation.13 | async-start | bytes 1843200 | tf_op jit(solution)/shard_map/reduce_scatter | solution.py:79
  156.4 3.6 copy-start.4
  160.0 4.0 copy-start.43
  164.0 6.0 %copy-start.12 = (bf16[640,1152]{0,1:T(8,128)(2,1)}, bf16[640,1152]{0,1:T(8,128)(2,1)S(1)}, u32[]{:S(2)}) copy-start(bf16[640,1152]{0,1:T(8,128)(2,1)S(1)} %fusion.11) | copy-start | bytes 4423684
  170.1 1.1 copy-start.44
  175.2 27.7 %copy-start.5 = (f32[640,1152]{0,1:T(8,128)S(1)}, f32[640,1152]{0,1:T(8,128)}, u32[]{:S(2)}) copy-start(f32[640,1152]{0,1:T(8,128)} %fusion.57) | copy-start | bytes 8847364
  175.2 58.3 %all-gather.12.cloned.1.call-start = ((), (), s32[]{:S(2)}) async-start(), calls=%async_computation.14 | async-start | bytes 1843200 | tf_op jit(solution)/shard_map/all_gather | solution.py:76
  213.1 50.6 %reduce-scatter.11.cloned.1.call-start = ((), (), s32[]{:S(2)}) async-start(), calls=%async_computation.11 | async-start | bytes 1843200 | tf_op jit(solution)/shard_map/reduce_scatter | solution.py:79
  213.2 6.7 %copy-start.13 = (bf16[640,1152]{0,1:T(8,128)(2,1)S(1)}, bf16[640,1152]{0,1:T(8,128)(2,1)}, u32[]{:S(2)}) copy-start(bf16[640,1152]{0,1:T(8,128)(2,1)} %copy-done.12) | copy-start | bytes 4423684
  219.8 5.6 copy-start.34
  219.8 118.9 %reduce-scatter.21.cloned.1.call-start = ((), (), s32[]{:S(2)}) async-start(), calls=%async_computation.18 | async-start | bytes 2985984 | tf_op jit(solution)/shard_map/reduce_scatter | solution.py:293
  225.3 186.7 %reduce-scatter.23.cloned.1.call-start = ((), (), s32[]{:S(2)}) async-start(), calls=%async_computation.19 | async-start | bytes 2985984 | tf_op jit(solution)/shard_map/reduce_scatter | solution.py:294
  231.2 4.7 copy-start.40
  231.2 244.9 %reduce-scatter.19.cloned.1.call-start = ((), (), s32[]{:S(2)}) async-start(), calls=%async_computation.17 | async-start | bytes 995328 | tf_op jit(solution)/shard_map/reduce_scatter | solution.py:292
  233.5 2.4 copy-start.35
  235.9 6.1 %copy-start.41 = (bf16[640,288]{0,1:T(8,128)(2,1)}, bf16[640,288]{0,1:T(8,128)(2,1)S(1)}, u32[]{:S(2)}) copy-start(bf16[640,288]{0,1:T(8,128)(2,1)S(1)} %convolution_convert_fusion.7) | copy-start | bytes 1105924
  235.9 1.9 copy-start.22
  237.9 4.3 slice-start
  237.9 5.1 slice-start.1
  243.0 1.0 copy-start.18
  246.0 259.4 %reduce-scatter.15.cloned.1.call-start = ((), (), s32[]{:S(2)}) async-start(), calls=%async_computation.15 | async-start | bytes 1843200 | tf_op jit(solution)/shard_map/reduce_scatter | solution.py:79
  246.1 1.7 copy-start.42
  247.8 4.4 copy-start.20
  247.8 4.4 copy-start.19
  247.8 4.4 copy-start.33
  252.2 3.3 copy-start.24
  252.2 3.5 copy-start.31
  252.2 3.5 copy-start.3
  255.4 2.2 copy-start.21
  255.5 324.8 %reduce-scatter.17.cloned.1.call-start = ((), (), s32[]{:S(2)}) async-start(), calls=%async_computation.16 | async-start | bytes 2985984 | tf_op jit(solution)/shard_map/reduce_scatter | solution.py:291
  257.7 6.0 %copy-start.7 = (f32[640,576]{0,1:T(8,128)S(1)}, f32[640,576]{0,1:T(8,128)}, u32[]{:S(2)}) copy-start(f32[640,576]{0,1:T(8,128)} %copy-done.6) | copy-start | bytes 4423684
  257.7 6.0 %copy-start.10 = (f32[640,288]{0,1:T(8,128)S(1)}, f32[640,288]{0,1:T(8,128)}, u32[]{:S(2)}) copy-start(f32[640,288]{0,1:T(8,128)} %get-tuple-element.52) | copy-start | bytes 2211844
  257.7 6.0 %copy-start.14 = (bf16[640,288]{0,1:T(8,128)(2,1)S(1)}, bf16[640,288]{0,1:T(8,128)(2,1)}, u32[]{:S(2)}) copy-start(bf16[640,288]{0,1:T(8,128)(2,1)} %reduce-scatter.9.cloned.1.call-done) | copy-start | bytes 1105924
  263.7 3.2 copy-start.25
  267.2 240.9 %copy-start.9 = (f32[640,288]{0,1:T(8,128)S(1)}, f32[640,288]{0,1:T(8,128)}, u32[]{:S(2)}) copy-start(f32[640,288]{0,1:T(8,128)} %get-tuple-element.30) | copy-start | bytes 2211844
  413.8 94.4 %copy-start.8 = (bf16[640,288]{0,1:T(8,128)(2,1)S(1)}, bf16[640,288]{0,1:T(8,128)(2,1)}, u32[]{:S(2)}) copy-start(bf16[640,288]{0,1:T(8,128)(2,1)} %reduce-scatter.13.cloned.1.call-done) | copy-start | bytes 1105924
  508.1 1.4 copy-start.23
  543.7 20.1 %copy-start.15 = (bf16[640,288]{0,1:T(8,128)(2,1)S(1)}, bf16[640,288]{0,1:T(8,128)(2,1)}, u32[]{:S(2)}) copy-start(bf16[640,288]{0,1:T(8,128)(2,1)} %reduce-scatter.15.cloned.1.call-done) | copy-start | bytes 1105924
  562.0 20.1 %copy-start.1 = (bf16[1152,1152]{1,0:T(8,128)(2,1)S(1)}, bf16[1152,1152]{1,0:T(8,128)(2,1)}, u32[]{:S(2)}) copy-start(bf16[1152,1152]{1,0:T(8,128)(2,1)} %param.30) | copy-start | bytes 7962628
Sparse Core Ops, SparseCore 0:
  13.8 29.6 all-gather.5
  86.0 27.8 reduce-scatter.8
  116.1 19.0 all-gather.9
  137.3 19.0 all-gather.7
  175.3 27.5 reduce-scatter.12
  213.2 20.2 all-gather.11
  236.1 27.5 reduce-scatter.10
  267.8 70.8 reduce-scatter.20
  342.4 69.5 reduce-scatter.22
  416.2 59.8 reduce-scatter.18
  478.9 26.4 reduce-scatter.14
  508.9 71.3 reduce-scatter.16
where the time goes:
time: 595 us; the launch traced here: 589 us
  waiting for transfers between devices  324 us (54%)
  matrix products  117 us (20%)
  blocking collectives  75 us (13%)
  other arithmetic  33.7 us (6%)
  local copies, waits for them, and re-layouts  23.8 us (4%)
  between operations  15.1 us (3%)
    reduce_scatter x4, waiting for transfers between devices, column_sum(): lax.psum_scatter(part_rows.astype(bf16), 'tp', scatter_dimension=1, tiled...  77.5 us
    reduce_scatter x1, waiting for transfers between devices, local(): lax.psum_scatter(hidden_weight_term, 'seq', scatter_dimension=0, tiled=True)  71.5 us
    reduce_scatter x1, waiting for transfers between devices, local(): lax.psum_scatter(output_weight_term, 'seq', scatter_dimension=1, tiled=True)  71.4 us
    reduce_scatter x1, waiting for transfers between devices, local(): lax.psum_scatter(proj_weight_term, 'seq', scatter_dimension=1, tiled=True)  62.3 us
    all_gather x1, blocking collectives, local(): small_all = lax.all_gather(small, 'seq', axis=0)  31.6 us
    all_gather x4, waiting for transfers between devices, whole_rows(): return lax.all_gather(part_rows, 'tp', axis=1, tiled=True)  28 us
    all_gather x1, blocking collectives, local(): mod_full = lax.all_gather(mod_own, 'tp', axis=2, tiled=True)  26.5 us
    dot_general x6, matrix products, exact_dot(): jnp.dot(left_mat, right_mat, precision=HIGHEST, preferred_element_type=jn...  19.7 us
  transfers between devices with their start and end apart: 12, of which 11 were waited for; matrix products, arithmetic and copies ran while one was open for 20% of the time, Pallas kernels for 0%

commit v1 on v0

--- a/solution.py
+++ b/solution.py
@@ -99,7 +99,12 @@
         jnp.einsum("wd,dcf->wcf", cond_own, ada_weight, preferred_element_type=f32)
         + ada_bias.astype(f32)[None]
     )
-    mod_full = lax.all_gather(mod_own, "tp", axis=2, tiled=True)
+    ring = [mod_own]
+    for hop in range(3):
+        ring.append(lax.ppermute(ring[-1], "tp", [(dev, (dev + 1) % 4) for dev in range(4)]))
+    mod_full = jnp.roll(
+        jnp.concatenate(ring[::-1], axis=2), (lax.axis_index("tp") + 1) * ring[0].shape[2], axis=2
+    )
 
     def row_full(stretch_id):
         return exact_dot(row_onehot, mod_full[:, stretch_id, :])

time: 595 us -> 570 us (0.958)
  blocking collectives: 75 us -> 48.2 us
  waiting for transfers between devices: 324 us -> 339 us
  local copies, waits for them, and re-layouts: 23.8 us -> 8.91 us
    all_gather x1 -> x0, blocking collectives: 26.5 us -> none  [local(): mod_full = lax.all_gather(mod_own, 'tp', axis=2, tiled=True)]
    slice x6 -> x1, local copies, waits for them, and re-layouts: 15 us -> 0.07 us  [the longest x5 14.9 us: row_full(): return exact_dot(row_onehot, mod_full[:, stretch_id, :])]
    ppermute x0 -> x3, waiting for transfers between devices: none -> 9.11 us  [local(): lax.ppermute(ring[-1], 'tp', [(dev, (dev + 1) % 4) for dev in range(4)])]
  transfers between devices with their start and end apart: 12 -> 15, of which waited for: 11 -> 15; matrix products, arithmetic and copies ran while one was open for 20% -> 18% of each run, Pallas kernels for 0% -> 0%
where the time goes in v1:
time: 570 us; the launch traced here: 566 us
  waiting for transfers between devices  339 us (59%)
  matrix products  118 us (21%)
  blocking collectives  48.2 us (8%)
  other arithmetic  33.7 us (6%)
  between operations  15.1 us (3%)
  local copies, waits for them, and re-layouts  8.91 us (2%)
    reduce_scatter x4, waiting for transfers between devices, column_sum(): lax.psum_scatter(part_rows.astype(bf16), 'tp', scatter_dimension=1, tiled...  79.6 us
    reduce_scatter x1, waiting for transfers between devices, local(): lax.psum_scatter(output_weight_term, 'seq', scatter_dimension=1, tiled=True)  71.5 us
    reduce_scatter x1, waiting for transfers between devices, local(): lax.psum_scatter(hidden_weight_term, 'seq', scatter_dimension=0, tiled=True)  71.2 us
    reduce_scatter x1, waiting for transfers between devices, local(): lax.psum_scatter(proj_weight_term, 'seq', scatter_dimension=1, tiled=True)  62.6 us
    all_gather x1, blocking collectives, local(): small_all = lax.all_gather(small, 'seq', axis=0)  31.7 us
    all_gather x4, waiting for transfers between devices, whole_rows(): return lax.all_gather(part_rows, 'tp', axis=1, tiled=True)  31.6 us
    dot_general x6, matrix products, exact_dot(): jnp.dot(left_mat, right_mat, precision=HIGHEST, preferred_element_type=jn...  20.8 us
    psum x2, blocking collectives, input_grads(): lax.psum((jnp.sum(scaled_grad, axis=1, keepdims=True) / model_width, jnp....  16.5 us
  transfers between devices with their start and end apart: 15, of which 15 were waited for; matrix products, arithmetic and copies ran while one was open for 18% of the time, Pallas kernels for 0%

profile of v1, /device:TPU:0, one launch (start us, length us, event | category | flops | bytes accessed | tf_op | source)
XLA Modules:
  0.0 565.6 jit_solution(3628967667367721034)
XLA Ops:
  9.3 2.4 fusion.24
  14.2 2.9 multiply_convert_fusion.4
  17.1 3.5 convolution_add_fusion.4
  22.4 2.2 collective-permute-done
  25.1 3.4 collective-permute-done.1
  29.3 3.5 collective-permute-done.2
  33.1 3.2 fusion.59
  36.4 1.8 convert_reduce_fusion.1
  38.2 1.8 fusion.13
  40.1 4.0 fusion.21
  44.1 1.9 add_convert_fusion
  46.8 6.5 %fusion.112 = (f32[4,640]{1,0:T(4,128)S(1)}, f32[4,640,640]{1,2,0:T(8,128)}) fusion(pred[640,640]{0,1:T(8,128)(4,1)} %broadcast_compare_fusion, bf16[640,4,72]{0,2,1:T(8,128)(2,1)S(1)} %bitcast.99, bf16[640,4,72]{0,2,1:T(8,128)(2,1)S(1)} %bitcast.97), kind=kOutput, calls=%fused_computation.191 | convolution fusion | flops 242483840 | bytes 7710720 | tf_op jit(solution)/shard_map/sub | solution.py:155
  53.3 3.7 fusion.38
  57.8 2.2 convolution_convert_fusion.5
  60.0 2.7 convert_reduce_fusion.4
  62.9 27.2 %reduce-scatter.9.cloned.1.call-done = bf16[640,288]{0,1:T(8,128)(2,1)} async-done(((bf16[640,1152]{0,1:T(8,128)(2,1)}), bf16[640,288]{0,1:T(8,128)(2,1)}) %reduce-scatter.9.cloned.1.call-update) | async-done | bytes 368656 | tf_op jit(solution)/shard_map/reduce_scatter | solution.py:79
  90.1 2.9 fusion.78
  93.3 3.9 fusion.57
  97.2 14.3 %all-gather.10.cloned.1.call-done = bf16[640,1152]{0,1:T(8,128)(2,1)} async-done(((bf16[640,288]{0,1:T(8,128)(2,1)}), bf16[640,1152]{0,1:T(8,128)(2,1)}) %all-gather.10.cloned.1.call-update) | async-done | bytes 1474576 | tf_op jit(solution)/shard_map/all_gather | solution.py:76
  111.4 6.1 %fusion.114 = f32[640,1152]{0,1:T(8,128)} fusion(bf16[1152,1152]{1,0:T(8,128)(2,1)} %param.32, bf16[640,1152]{0,1:T(8,128)(2,1)} %all-gather.10.cloned.1.call-done), kind=kOutput, calls=%fused_computation.193 | convolution fusion | flops 1698693120 | bytes 7077888 | tf_op jit(solution)/shard_map/rd,fd->rf/dot_general | solution.py:185
  117.6 15.1 %all-gather.8.cloned.1.call-done = bf16[640,1152]{0,1:T(8,128)(2,1)} async-done(((bf16[640,288]{0,1:T(8,128)(2,1)}), bf16[640,1152]{0,1:T(8,128)(2,1)}) %all-gather.8.cloned.1.call-update) | async-done | bytes 1474576 | tf_op jit(solution)/shard_map/all_gather | solution.py:76
  132.7 1.8 convert_reduce_fusion
  134.4 1.8 fusion.12
  136.3 4.0 fusion.11
  140.4 6.0 %convert_reduce_fusion.2 = (f32[1152]{0:T(1024)S(1)}, bf16[640,1152]{0,1:T(8,128)(2,1)S(1)}, f32[640,1152]{0,1:T(8,128)}) fusion(f32[640,1152]{0,1:T(8,128)S(1)} %copy-done.44, f32[1152]{0:T(1024)S(1)} %convert_element_type.178, bf16[640,1152]{0,1:T(8,128)(2,1)S(1)} %fusion.11, bf16[1152,1152]{1,0:T(8,128)(2,1)S(1)} %copy-done), kind=kOutput, calls=%fused_computation.42 | convolution fusion | flops 1715649408 | bytes 11510784 | tf_op jit(solution)/shard_map/dot_general | solution.py:171
  146.4 1.1 copy-done.45
  147.5 3.9 convolution_convert_fusion.3
  151.5 3.4 fusion.4
  154.9 24.3 %reduce-scatter.13.cloned.1.call-done = bf16[640,288]{0,1:T(8,128)(2,1)} async-done(((bf16[640,1152]{0,1:T(8,128)(2,1)}), bf16[640,288]{0,1:T(8,128)(2,1)}) %reduce-scatter.13.cloned.1.call-update) | async-done | bytes 368656 | tf_op jit(solution)/shard_map/reduce_scatter | solution.py:79
  179.2 1.4 fusion.74
  180.6 5.9 %all-reduce.1 = (f32[640]{0:T(1024)S(1)}, f32[640]{0:T(1024)S(1)}) all-reduce(f32[640]{0:T(1024)S(1)} %get-tuple-element.53, f32[640]{0:T(1024)S(1)} %get-tuple-element.54), channel_id=1, replica_groups=mesh['seq'=8,'tp'=4] {'tp'}, use_global_device_ids=true, to_apply=%region_16.17 | all-reduce | flops 1280 | bytes 10240 | tf_op jit(solution)/shard_map/psum | solution.py:119
  186.5 2.9 convert_reduce_fusion.5
  189.5 6.5 %convolution_convert_fusion.4 = bf16[640,1152]{0,1:T(8,128)(2,1)} fusion(bf16[1152,1152]{1,0:T(8,128)(2,1)} %param.32, f32[640,1152]{0,1:T(8,128)} %get-tuple-element.50), kind=kOutput, calls=%fused_computation.28 | convolution fusion | flops 1706065920 | bytes 7077888 | tf_op jit(solution)/shard_map/dot_general | solution.py:176
  196.1 5.4 convolution_convert_fusion.1
  201.6 5.8 %convolution_convert_fusion = bf16[1152,1152]{0,1:T(8,128)(2,1)} fusion(bf16[640,1152]{0,1:T(8,128)(2,1)S(1)} %copy-done.35, f32[640,1152]{0,1:T(8,128)} %get-tuple-element.50), kind=kOutput, calls=%fused_computation.1 | convolution fusion | flops 1706655744 | bytes 7077888 | tf_op jit(solution)/shard_map/rf,rd->fd/dot_general | solution.py:182
  207.7 2.1 all-gather.12.cloned.1.call-done
  209.8 2.4 convolution_convert_fusion.7
  212.3 1.9 convolution_convert_fusion.6
  214.2 4.1 multiply_reduce_fusion
  220.3 2.0 fusion.37
  222.4 1.7 fusion.36
  224.2 4.3 fusion.41
  228.5 3.2 fusion.9
  232.1 1.9 fusion.2
  234.0 5.5 convolution_convert_fusion.2
  240.0 3.2 fusion.35
  243.5 71.2 %reduce-scatter.21.cloned.1.call-done = bf16[144,1152]{1,0:T(8,128)(2,1)} async-done(((bf16[1152,1152]{1,0:T(8,128)(2,1)}), bf16[144,1152]{1,0:T(8,128)(2,1)}) %reduce-scatter.21.cloned.1.call-update) | async-done | bytes 331792 | tf_op jit(solution)/shard_map/reduce_scatter | solution.py:298
  314.6 1.9 convert_element_type.205
  316.5 71.5 %reduce-scatter.23.cloned.1.call-done = bf16[1152,144]{0,1:T(8,128)(2,1)} async-done(((bf16[1152,1152]{0,1:T(8,128)(2,1)}), bf16[1152,144]{0,1:T(8,128)(2,1)}) %reduce-scatter.23.cloned.1.call-update) | async-done | bytes 331792 | tf_op jit(solution)/shard_map/reduce_scatter | solution.py:299
  388.1 1.9 convert_element_type.207
  389.9 62.6 %reduce-scatter.19.cloned.1.call-done = bf16[288,144]{0,1:T(8,128)(2,1)} async-done(((bf16[288,1152]{0,1:T(8,128)(2,1)}), bf16[288,144]{0,1:T(8,128)(2,1)}) %reduce-scatter.19.cloned.1.call-update) | async-done | bytes 82960 | tf_op jit(solution)/shard_map/reduce_scatter | solution.py:297
  452.5 1.6 convert_element_type.203
  454.1 27.7 %reduce-scatter.15.cloned.1.call-done = bf16[640,288]{0,1:T(8,128)(2,1)} async-done(((bf16[640,1152]{0,1:T(8,128)(2,1)}), bf16[640,288]{0,1:T(8,128)(2,1)}) %reduce-scatter.15.cloned.1.call-update) | async-done | bytes 368656 | tf_op jit(solution)/shard_map/reduce_scatter | solution.py:79
  482.8 1.6 fusion.75
  484.7 1.2 fusion.48
  486.1 2.3 fusion.64
  488.6 31.7 %all-gather = f32[73728]{0:T(1024)S(1)} all-gather(f32[9216]{0:T(1024)S(1)} %concatenate.28), channel_id=2, replica_groups=mesh['seq'=8,'tp'=4] {'seq'}, dimensions={0}, use_global_device_ids=true | all-gather | bytes 331776 | tf_op jit(solution)/shard_map/all_gather | solution.py:258
  522.6 2.0 convolution_bitcast_fusion.1
  524.7 10.6 %all-reduce = (f32[640]{0:T(1024)S(1)}, f32[640]{0:T(1024)S(1)}, f32[32,144]{1,0:T(8,128)S(1)}) all-reduce(f32[640]{0:T(1024)S(1)} %broadcast_multiply_fusion, f32[640]{0:T(1024)S(1)} %broadcast_multiply_fusion.1, f32[32,144]{1,0:T(8,128)S(1)} %convolution_bitcast_fusion.1), channel_id=1, replica_groups=mesh['seq'=8,'tp'=4] {'tp'}, use_global_device_ids=true, to_apply=%region_22.23 | all-reduce | flops 5888 | bytes 47104 | tf_op jit(solution)/shard_map/psum | solution.py:119
  536.0 2.1 fusion.73
  538.1 1.8 fusion.61
  540.0 3.6 fusion.34
  543.5 13.1 %reduce-scatter.17.cloned.1.call-done = bf16[144,3,288]{2,0,1:T(8,128)(2,1)} async-done(((bf16[1152,3,288]{2,0,1:T(8,128)(2,1)}), bf16[144,3,288]{2,0,1:T(8,128)(2,1)}) %reduce-scatter.17.cloned.1.call-update) | async-done | bytes 248848 | tf_op jit(solution)/shard_map/reduce_scatter | solution.py:296
  556.6 1.9 convert_element_type.201
  (172 shorter events, 18.3 us)
Async XLA Ops:
  7.2 133.1 %copy-start = (bf16[1152,1152]{1,0:T(8,128)(2,1)S(1)}, bf16[1152,1152]{1,0:T(8,128)(2,1)}, u32[]{:S(2)}) copy-start(bf16[1152,1152]{1,0:T(8,128)(2,1)} %param.30) | copy-start | bytes 7962628
  7.2 29.2 %all-gather.6.cloned.1.call-start = ((), (), s32[]{:S(2)}) async-start(), calls=%async_computation.8 | async-start | bytes 1843200 | tf_op jit(solution)/shard_map/all_gather | solution.py:76
  9.3 4.4 copy-start.38
  9.3 4.4 copy-start.28
  9.3 4.8 copy-start.30
  11.8 1.1 copy-start.6
  13.7 76.4 %reduce-scatter.9.cloned.1.call-start = ((), (), s32[]{:S(2)}) async-start(), calls=%async_computation.9 | async-start | bytes 1843200 | tf_op jit(solution)/shard_map/reduce_scatter | solution.py:79
  14.2 6.8 %copy-start.39 = (s32[32]{0:T(128)S(1)}, s32[32]{0:T(128)}, u32[]{:S(2)}) copy-start(s32[32]{0:T(128)} %param.20) | copy-start | bytes 388
  14.2 10.8 %copy-start.27 = (bf16[2,288]{1,0:T(2,128)(2,1)S(1)}, bf16[2,288]{1,0:T(2,128)(2,1)}, u32[]{:S(2)}) copy-start(bf16[2,288]{1,0:T(2,128)(2,1)} %param.27) | copy-start | bytes 3460
  20.5 4.0 collective-permute-start
  24.6 3.9 collective-permute-start.1
  28.5 4.3 collective-permute-start.2
  33.1 6.9 %copy-start.22 = (f32[4,6,2304]{2,0,1:T(4,128)}, f32[4,6,2304]{2,0,1:T(4,128)S(1)}, u32[]{:S(2)}) copy-start(f32[4,6,2304]{2,0,1:T(4,128)S(1)} %concatenate.26) | copy-start | bytes 663556
  36.4 3.6 copy-start.2
  40.1 4.0 copy-start.33
  44.1 1.9 copy-start.11
  46.8 6.5 %copy-start.16 = (bf16[640,1,288]{0,2,1:T(8,128)(2,1)}, bf16[640,1,288]{0,2,1:T(8,128)(2,1)S(1)}, u32[]{:S(2)}) copy-start(bf16[640,1,288]{0,2,1:T(8,128)(2,1)S(1)} %get-tuple-element.34) | copy-start | bytes 1105924
  46.8 6.5 %copy-start.17 = (bf16[640,1,288]{0,2,1:T(8,128)(2,1)}, bf16[640,1,288]{0,2,1:T(8,128)(2,1)S(1)}, u32[]{:S(2)}) copy-start(bf16[640,1,288]{0,2,1:T(8,128)(2,1)S(1)} %get-tuple-element.35) | copy-start | bytes 1105924
  53.3 4.5 copy-start.37
  57.0 0.7 copy-start.40
  57.8 5.1 copy-start.31
  60.0 33.3 %copy-start.29 = (bf16[1152]{0:T(1024)(128)(2,1)S(1)}, bf16[1152]{0:T(1024)(128)(2,1)}, u32[]{:S(2)}) copy-start(bf16[1152]{0:T(1024)(128)(2,1)} %param.31) | copy-start | bytes 6916
  60.0 51.5 %all-gather.10.cloned.1.call-start = ((), (), s32[]{:S(2)}) async-start(), calls=%async_computation.12 | async-start | bytes 1843200 | tf_op jit(solution)/shard_map/all_gather | solution.py:76
  62.8 69.9 %all-gather.8.cloned.1.call-start = ((), (), s32[]{:S(2)}) async-start(), calls=%async_computation.10 | async-start | bytes 1843200 | tf_op jit(solution)/shard_map/all_gather | solution.py:76
  93.0 86.2 %reduce-scatter.13.cloned.1.call-start = ((), (), s32[]{:S(2)}) async-start(), calls=%async_computation.13 | async-start | bytes 1843200 | tf_op jit(solution)/shard_map/reduce_scatter | solution.py:79
  132.7 3.6 copy-start.4
  136.3 4.1 copy-start.44
  140.3 6.1 %copy-start.12 = (bf16[640,1152]{0,1:T(8,128)(2,1)}, bf16[640,1152]{0,1:T(8,128)(2,1)S(1)}, u32[]{:S(2)}) copy-start(bf16[640,1152]{0,1:T(8,128)(2,1)S(1)} %fusion.11) | copy-start | bytes 4423684
  146.4 1.1 copy-start.45
  151.5 27.7 %copy-start.5 = (f32[640,1152]{0,1:T(8,128)S(1)}, f32[640,1152]{0,1:T(8,128)}, u32[]{:S(2)}) copy-start(f32[640,1152]{0,1:T(8,128)} %fusion.57) | copy-start | bytes 8847364
  151.5 58.3 %all-gather.12.cloned.1.call-start = ((), (), s32[]{:S(2)}) async-start(), calls=%async_computation.14 | async-start | bytes 1843200 | tf_op jit(solution)/shard_map/all_gather | solution.py:76
  189.4 50.6 %reduce-scatter.11.cloned.1.call-start = ((), (), s32[]{:S(2)}) async-start(), calls=%async_computation.11 | async-start | bytes 1843200 | tf_op jit(solution)/shard_map/reduce_scatter | solution.py:79
  189.5 6.6 %copy-start.13 = (bf16[640,1152]{0,1:T(8,128)(2,1)S(1)}, bf16[640,1152]{0,1:T(8,128)(2,1)}, u32[]{:S(2)}) copy-start(bf16[640,1152]{0,1:T(8,128)(2,1)} %copy-done.12) | copy-start | bytes 4423684
  196.0 5.6 copy-start.35
  196.0 118.6 %reduce-scatter.21.cloned.1.call-start = ((), (), s32[]{:S(2)}) async-start(), calls=%async_computation.18 | async-start | bytes 2985984 | tf_op jit(solution)/shard_map/reduce_scatter | solution.py:298
  201.5 186.5 %reduce-scatter.23.cloned.1.call-start = ((), (), s32[]{:S(2)}) async-start(), calls=%async_computation.19 | async-start | bytes 2985984 | tf_op jit(solution)/shard_map/reduce_scatter | solution.py:299
  207.4 4.8 copy-start.41
  207.4 245.1 %reduce-scatter.19.cloned.1.call-start = ((), (), s32[]{:S(2)}) async-start(), calls=%async_computation.17 | async-start | bytes 995328 | tf_op jit(solution)/shard_map/reduce_scatter | solution.py:297
  209.8 2.4 copy-start.36
  212.2 6.1 %copy-start.42 = (bf16[640,288]{0,1:T(8,128)(2,1)}, bf16[640,288]{0,1:T(8,128)(2,1)S(1)}, u32[]{:S(2)}) copy-start(bf16[640,288]{0,1:T(8,128)(2,1)S(1)} %convolution_convert_fusion.7) | copy-start | bytes 1105924
  212.2 1.9 copy-start.23
  214.2 4.3 slice-start
  214.2 5.1 slice-start.1
  219.3 1.0 copy-start.18
  222.3 259.5 %reduce-scatter.15.cloned.1.call-start = ((), (), s32[]{:S(2)}) async-start(), calls=%async_computation.15 | async-start | bytes 1843200 | tf_op jit(solution)/shard_map/reduce_scatter | solution.py:79
  222.4 1.7 copy-start.43
  224.1 4.4 copy-start.20
  224.1 4.4 copy-start.19
  224.1 4.4 copy-start.34
  228.5 3.3 copy-start.25
  228.5 3.5 copy-start.32
  228.5 3.5 copy-start.3
  231.7 2.2 copy-start.21
  231.8 324.9 %reduce-scatter.17.cloned.1.call-start = ((), (), s32[]{:S(2)}) async-start(), calls=%async_computation.16 | async-start | bytes 2985984 | tf_op jit(solution)/shard_map/reduce_scatter | solution.py:296
  233.9 6.0 %copy-start.7 = (f32[640,576]{0,1:T(8,128)S(1)}, f32[640,576]{0,1:T(8,128)}, u32[]{:S(2)}) copy-start(f32[640,576]{0,1:T(8,128)} %copy-done.6) | copy-start | bytes 4423684
  233.9 6.0 %copy-start.10 = (f32[640,288]{0,1:T(8,128)S(1)}, f32[640,288]{0,1:T(8,128)}, u32[]{:S(2)}) copy-start(f32[640,288]{0,1:T(8,128)} %get-tuple-element.48) | copy-start | bytes 2211844
  233.9 6.0 %copy-start.14 = (bf16[640,288]{0,1:T(8,128)(2,1)S(1)}, bf16[640,288]{0,1:T(8,128)(2,1)}, u32[]{:S(2)}) copy-start(bf16[640,288]{0,1:T(8,128)(2,1)} %reduce-scatter.9.cloned.1.call-done) | copy-start | bytes 1105924
  240.0 3.2 copy-start.26
  243.5 241.0 %copy-start.9 = (f32[640,288]{0,1:T(8,128)S(1)}, f32[640,288]{0,1:T(8,128)}, u32[]{:S(2)}) copy-start(f32[640,288]{0,1:T(8,128)} %get-tuple-element.30) | copy-start | bytes 2211844
  389.9 94.8 %copy-start.8 = (bf16[640,288]{0,1:T(8,128)(2,1)S(1)}, bf16[640,288]{0,1:T(8,128)(2,1)}, u32[]{:S(2)}) copy-start(bf16[640,288]{0,1:T(8,128)(2,1)} %reduce-scatter.13.cloned.1.call-done) | copy-start | bytes 1105924
  484.5 1.4 copy-start.24
  520.3 19.7 %copy-start.15 = (bf16[640,288]{0,1:T(8,128)(2,1)S(1)}, bf16[640,288]{0,1:T(8,128)(2,1)}, u32[]{:S(2)}) copy-start(bf16[640,288]{0,1:T(8,128)(2,1)} %reduce-scatter.15.cloned.1.call-done) | copy-start | bytes 1105924
  538.1 20.4 %copy-start.1 = (bf16[1152,1152]{1,0:T(8,128)(2,1)S(1)}, bf16[1152,1152]{1,0:T(8,128)(2,1)}, u32[]{:S(2)}) copy-start(bf16[1152,1152]{1,0:T(8,128)(2,1)} %param.30) | copy-start | bytes 7962628
Sparse Core Ops, SparseCore 0:
  13.8 22.5 all-gather.5
  60.1 29.9 reduce-scatter.8
  92.3 19.1 all-gather.9
  113.5 19.0 all-gather.7
  151.6 27.5 reduce-scatter.12
  189.5 20.2 all-gather.11
  212.4 27.5 reduce-scatter.10
  244.1 70.5 reduce-scatter.20
  318.3 69.6 reduce-scatter.22
  392.3 60.2 reduce-scatter.18
  455.3 26.4 reduce-scatter.14
  485.3 71.2 reduce-scatter.16
